TPU v7x, 512 devices: a whole 4x4x16 slice. The times are simulated.
512 devices in a mesh: group: 64 (over z, y_hi, core), tp: 8 (over x, y_lo).
Axes of the slice: x: 4, y: 4 (y_hi: 2, y_lo: 2; y = y_hi * 2 + y_lo), z: 16, core: 2. Of those that a mesh axis runs over, the one named last changes fastest.
Arguments:
- queries: bfloat16 [4096, 2048], P('group', 'tp'), may hold values from -22 to 22
- new_kv: bfloat16 [4096, 1024], P('group', 'tp'), may hold values from -6 to 6
- local_cache: bfloat16 [16384, 1024], P('group', 'tp'), may hold values from -6 to 6
- remote_pool: bfloat16 [32768, 1024], P('group', 'tp'), may hold values from -6 to 6
- page_index: int32 [64, 64], P('group'), may hold values from 0 to 63, each once within a row
- lengths: int32 [64], P('group'), may hold values from 256 to 768, as said below
- sinks: float32 [32], P('tp'), may hold values from 4 to 8
- out_weight: bfloat16 [2048, 2880], P('tp'), may hold values from -0.125 to 0.125
- residual: bfloat16 [4096, 2880], P('group', 'tp'), may hold values from -6 to 6
- norm_gain: float32 [2880], replicated, may hold values from 0.5 to 2
- routes: int32 [4096, 4], P('group'), may hold values from 0 to 31, all different within a row; in each aligned block of 64 rows (0 to 63, 64 to 127, ...) at most 10 rows name the same one
- route_weights: float32 [4096, 4], P('group'), may hold values from 0.1 to 1
- expert_gate: bfloat16 [64, 2880, 1440], P('group', None, 'tp'), may hold values from -0.109375 to 0.109375
- expert_up: bfloat16 [64, 2880, 1440], P('group', None, 'tp'), may hold values from -0.109375 to 0.109375
- expert_down: bfloat16 [64, 1440, 2880], P('group', None, 'tp'), may hold values from -0.109375 to 0.109375
Outputs:
- layer_out: bfloat16 [4096, 2880], P('group', 'tp')
Inputs may be any that keep to these rules, and one draw needn't show every extreme that they name: `lengths`: every request has at least 256 cached positions; some request has exactly 256, some exactly 768. `routes`: within the rows of one request no expert is named by more than 10 rows. `page_index`: each row is a permutation.
All inputs are finite; a program needn't handle non-finite values.
Results may differ from a plain program's by a relative error of at most 0.013.
Values may be sent and summed in bfloat16 or wider, within the bound.
A program may use at most 64 MiB of HBM per device.

v0:
```python
import jax
import jax.numpy as jnp
from jax import lax
from jax.sharding import PartitionSpec as P

HEAD = 64
THETA = 150000.0
ALPHA = 1.702
EPSILON = 1e-05


def rotate(values, positions):
    half_dim = values.shape[-1] // 2
    inverse = THETA ** (-2.0 * jnp.arange(half_dim, dtype=jnp.float32) / values.shape[-1])
    angles = positions[:, None, None] * inverse[None, None, :]
    cosine = jnp.cos(angles)
    sine_part = jnp.sin(angles)
    first_part = values[..., :half_dim]
    second_part = values[..., half_dim:]
    return jnp.concatenate(
        [
            first_part * cosine - second_part * sine_part,
            second_part * cosine + first_part * sine_part,
        ],
        axis=-1,
    )


def attend(query_rows, kv_rows, cache_kv, cache_valid, sinks, length):
    block_len = query_rows.shape[0]
    kv_heads = kv_rows.shape[1] // (2 * HEAD)
    query_heads = query_rows.shape[1] // HEAD
    group_size = query_heads // kv_heads
    positions = (length + jnp.arange(block_len, dtype=jnp.int32)).astype(jnp.float32)
    query_rot = rotate(
        query_rows.astype(jnp.float32).reshape(block_len, query_heads, HEAD), positions
    ).astype(jnp.bfloat16)
    kv_parts = kv_rows.reshape(block_len, kv_heads, 2, HEAD)
    key_rot = rotate(kv_parts[:, :, 0].astype(jnp.float32), positions).astype(jnp.bfloat16)
    cache_parts = cache_kv.reshape(cache_kv.shape[0], kv_heads, 2, HEAD)
    all_keys = jnp.concatenate([cache_parts[:, :, 0], key_rot], axis=0)
    all_values = jnp.concatenate([cache_parts[:, :, 1], kv_parts[:, :, 1]], axis=0)
    token_order = jnp.arange(block_len, dtype=jnp.int32)
    causal = token_order[None, :] <= token_order[:, None]
    allowed = jnp.concatenate(
        [jnp.broadcast_to(cache_valid[None, :], (block_len, cache_valid.shape[0])), causal], axis=1
    )
    row_allowed = jnp.repeat(allowed, group_size, axis=0)
    score_scale = HEAD ** (-0.5)
    query_block = query_rot.reshape(block_len * group_size, HEAD)
    scores = (
        jnp.dot(query_block, all_keys[:, 0].T, preferred_element_type=jnp.float32) * score_scale
    )
    scores = jnp.where(row_allowed, scores, -jnp.inf)
    sink_rows = jnp.tile(sinks, block_len)
    row_max = jnp.maximum(jnp.max(scores, axis=1), sink_rows)
    weights = jnp.exp(scores - row_max[:, None])
    denominator = jnp.sum(weights, axis=1) + jnp.exp(sink_rows - row_max)
    blended = (
        jnp.dot(weights.astype(jnp.bfloat16), all_values[:, 0], preferred_element_type=jnp.float32)
        / denominator[:, None]
    )
    outputs = blended.astype(jnp.bfloat16).reshape(block_len, group_size * HEAD)
    return outputs


def on_device(
    queries,
    new_kv,
    local_cache,
    remote_pool,
    page_index,
    lengths,
    sinks,
    out_weight,
    residual,
    norm_gain,
    routes,
    route_weights,
    expert_gate,
    expert_up,
    expert_down,
):
    groups = lax.axis_size("group")
    lane_count = remote_pool.shape[1]
    local_len = local_cache.shape[0]
    fetched = lax.all_to_all(
        remote_pool.reshape(groups, -1, lane_count),
        "group",
        split_axis=0,
        concat_axis=0,
        tiled=True,
    )
    page_len = fetched.shape[1]
    length = lengths[0]
    offsets = jnp.arange(page_len, dtype=jnp.int32)
    remote_pos = local_len + page_index[0][:, None] * page_len + offsets[None, :]
    cache_valid = jnp.concatenate(
        [jnp.ones((local_len,), jnp.bool_), (remote_pos < length).reshape(-1)]
    )
    cache_kv = jnp.concatenate([local_cache, fetched.reshape(-1, lane_count)], axis=0)
    attended = attend(queries, new_kv, cache_kv, cache_valid, sinks, length)
    width = residual.shape[1]
    start = lax.axis_index("tp") * width
    own_gain = lax.dynamic_slice_in_dim(norm_gain, start, width, 0)
    partial_sum = jnp.dot(attended, out_weight, preferred_element_type=jnp.float32)
    own_cols = lax.dynamic_slice_in_dim(partial_sum, start, width, 1) + residual.astype(jnp.float32)
    partial_sum = lax.dynamic_update_slice_in_dim(partial_sum, own_cols, start, 1)
    hidden_state = lax.psum(partial_sum, "tp")
    mean_square = jnp.mean(hidden_state * hidden_state, axis=1, keepdims=True)
    own_state = lax.dynamic_slice_in_dim(hidden_state, start, width, 1)
    normed_own = (own_state * lax.rsqrt(mean_square + EPSILON) * own_gain).astype(jnp.bfloat16)
    block_len = normed_own.shape[0]
    top_count = routes.shape[1]
    experts = groups // 2
    capacity = 5 * block_len * top_count // (4 * experts)
    member = jnp.any(
        routes[:, :, None] == jnp.arange(experts, dtype=jnp.int32)[None, None, :], axis=1
    ).astype(jnp.int32)
    slot_rank = jnp.cumsum(member, axis=0) - member
    slot_hit = member[:, :, None] * (
        slot_rank[:, :, None] == jnp.arange(capacity, dtype=jnp.int32)[None, None, :]
    ).astype(jnp.int32)
    slot_token = jnp.sum(slot_hit * jnp.arange(block_len, dtype=jnp.int32)[:, None, None], axis=0)
    slot_valid = jnp.sum(slot_hit, axis=0)
    send_own = jnp.take(normed_own, slot_token.reshape(-1), axis=0) * slot_valid.reshape(
        -1, 1
    ).astype(jnp.bfloat16)
    hidden_part = expert_gate.shape[2]
    gate_and_up = jnp.concatenate([expert_gate[0], expert_up[0]], axis=1)
    outgoing = send_own
    feature_count = outgoing.shape[1]
    outgoing = outgoing.reshape(experts, 1, capacity, feature_count)
    outgoing = jnp.broadcast_to(outgoing, (experts, 2, capacity, feature_count)).reshape(
        groups, capacity, feature_count
    )
    whole = lax.all_gather(
        lax.all_to_all(outgoing, "group", split_axis=0, concat_axis=0, tiled=True),
        "tp",
        axis=2,
        tiled=True,
    )
    sources, slot_count, features = whole.shape
    flat_rows = whole.reshape(sources * slot_count, features)
    both = jnp.dot(flat_rows, gate_and_up, preferred_element_type=jnp.float32)
    gate_val = both[:, :hidden_part]
    up_val = both[:, hidden_part:]
    active = (gate_val * jax.nn.sigmoid(ALPHA * gate_val) * (up_val + 1.0)).astype(jnp.bfloat16)
    joined = lax.all_gather(active, "tp", axis=1, tiled=True)
    result = jnp.dot(joined, expert_down[0], preferred_element_type=jnp.float32).astype(
        jnp.bfloat16
    )
    returned = result.reshape(sources, slot_count, result.shape[1])
    arrived = lax.all_to_all(returned, "group", split_axis=0, concat_axis=0, tiled=True)
    halves = arrived.reshape(experts, 2, capacity, width).astype(jnp.float32)
    summed = (halves[:, 0] + halves[:, 1]).reshape(experts * capacity, width)
    rank_at = jnp.take_along_axis(slot_rank, routes, axis=1)
    picked = jnp.take(summed, (routes * capacity + rank_at).reshape(-1), axis=0).reshape(
        block_len, top_count, width
    )
    mixing = route_weights / jnp.sum(route_weights, axis=1, keepdims=True)
    moe_out = jnp.sum(mixing[:, :, None] * picked, axis=1)
    return (own_state + moe_out).astype(jnp.bfloat16)


def solution(mesh):
    return jax.shard_map(
        on_device,
        mesh=mesh,
        in_specs=(
            P("group", "tp"),
            P("group", "tp"),
            P("group", "tp"),
            P("group", "tp"),
            P("group", None),
            P("group"),
            P("tp"),
            P("tp", None),
            P("group", "tp"),
            P(),
            P("group", None),
            P("group", None),
            P("group", None, "tp"),
            P("group", None, "tp"),
            P("group", None, "tp"),
        ),
        out_specs=P("group", "tp"),
        check_vma=False,
    )
```

profile of v0, /device:TPU:2, one launch (start us, length us, event | category | flops | bytes accessed | tf_op | source)
XLA Modules:
  0.0 590.5 jit_solution(3634151493439080288)
XLA Ops:
  6.5 18.9 %all-to-all-start = ((bf16[64,8,128]{2,1,0:T(8,128)(2,1)}), bf16[64,8,128]{2,1,0:T(8,128)(2,1)S(1)}, u32[]{:S(2)}, u32[]{:S(2)}) async-start(bf16[64,8,128]{2,1,0:T(8,128)(2,1)} %bitcast.65), calls=%async_computation | async-start | bytes 262144 | tf_op jit(solution)/shard_map/all_to_all | solution.py:87
  26.2 0.9 reshape.390
  27.0 0.8 copy.147
  27.9 0.9 copy.144
  29.0 0.7 add_bitcast_fusion
  31.2 0.8 dynamic_slice.11
  32.4 11.6 %all-to-all-done = bf16[64,8,128]{2,1,0:T(8,128)(2,1)S(1)} async-done(((bf16[64,8,128]{2,1,0:T(8,128)(2,1)}), bf16[64,8,128]{2,1,0:T(8,128)(2,1)S(1)}, u32[]{:S(2)}, u32[]{:S(2)}) %all-to-all-start) | async-done | bytes 131104 | tf_op jit(solution)/shard_map/all_to_all | solution.py:87
  44.1 0.7 slice_maximum_fusion
  46.6 0.6 fusion.41
  47.3 1.1 dynamic_update_slice.3
  48.4 0.9 copy-done.1
  50.3 78.5 %all-reduce.3.cloned.1.call-done = f32[64,2880]{1,0:T(8,128)} async-done(((f32[64,2880]{1,0:T(8,128)}), f32[64,2880]{1,0:T(8,128)}) %all-reduce.3.cloned.1.call-update) | async-done | bytes 737296 | tf_op jit(solution)/shard_map/psum | solution.py:109
  128.8 1.3 multiply_reduce_fusion
  130.1 1.0 multiply_convert_fusion
  131.1 2.0 gather_fusion
  133.6 59.9 %all_to_all.15 = bf16[64,10,360]{2,1,0:T(8,128)(2,1)S(1)} all-to-all(bf16[64,10,360]{2,1,0:T(8,128)(2,1)S(1)} %bitcast.58), channel_id=1, replica_groups=mesh['group'=64,'tp'=8] {'group'}, dimensions={0} | all-to-all | bytes 921600 | tf_op jit(solution)/shard_map/all_to_all | solution.py:138
  193.5 2.0 copy.165
  195.8 231.1 %all-gather.4.cloned.1.call-done = bf16[64,10,2880]{0,1,2:T(8,128)(2,1)} async-done(((bf16[64,10,360]{0,1,2:T(8,128)(2,1)}), bf16[64,10,2880]{0,1,2:T(8,128)(2,1)}) %all-gather.4.cloned.1.call-update) | async-done | bytes 3686416 | tf_op jit(solution)/shard_map/all_gather | solution.py:137
  426.8 17.0 %copy.166 = bf16[64,10,2880]{2,1,0:T(8,128)(2,1)} copy(bf16[64,10,2880]{0,1,2:T(8,128)(2,1)} %all-gather.4.cloned.1.call-done) | data formatting | bytes 7372800 | tf_op jit(solution)/shard_map/all_gather | solution.py:137
  443.8 7.9 %reshape.386 = bf16[640,2880]{1,0:T(8,128)(2,1)} reshape(bf16[64,10,2880]{2,1,0:T(8,128)(2,1)} %copy.166) | data formatting | bytes 7372800 | tf_op jit(solution)/shard_map/reshape | solution.py:144
  451.7 4.3 fusion
  456.0 0.9 fusion.14
  456.8 55.6 %all-gather.6.cloned.1.call-done = bf16[8,180,640]{2,1,0:T(8,128)(2,1)} async-done(((bf16[1,180,640]{2,1,0:T(8,128)(2,1)}), bf16[8,180,640]{2,1,0:T(8,128)(2,1)}) %all-gather.6.cloned.1.call-update) | async-done | bytes 1843216 | tf_op jit(solution)/shard_map/all_gather | solution.py:149
  512.5 1.7 reshape.421
  514.2 3.1 convolution_convert_fusion
  517.3 1.3 copy.167
  518.5 1.1 reshape.387
  519.6 16.0 %all-to-all-start.2 = ((bf16[64,10,360]{2,1,0:T(8,128)(2,1)}), bf16[64,10,360]{2,1,0:T(8,128)(2,1)S(1)}, u32[]{:S(2)}, u32[]{:S(2)}) async-start(bf16[64,10,360]{2,1,0:T(8,128)(2,1)} %reshape.387), calls=%async_computation.2 | async-start | bytes 1572864 | tf_op jit(solution)/shard_map/all_to_all | solution.py:154
  535.9 1.9 gather_fusion.2
  538.5 42.0 %all-to-all-done.2 = bf16[64,10,360]{2,1,0:T(8,128)(2,1)S(1)} async-done(((bf16[64,10,360]{2,1,0:T(8,128)(2,1)}), bf16[64,10,360]{2,1,0:T(8,128)(2,1)S(1)}, u32[]{:S(2)}, u32[]{:S(2)}) %all-to-all-start.2) | async-done | bytes 460832 | tf_op jit(solution)/shard_map/all_to_all | solution.py:154
  580.9 1.0 gather_fusion.1
  582.4 1.6 add_convert_fusion.1
  (86 shorter events, 7.3 us)
Async XLA Ops:
  6.5 40.0 %copy-start = (bf16[256,2880]{0,1:T(8,128)(2,1)S(1)}, bf16[256,2880]{0,1:T(8,128)(2,1)}, u32[]{:S(2)}) copy-start(bf16[256,2880]{0,1:T(8,128)(2,1)} %param.22) | copy-start | bytes 4423684
  6.5 24.1 %copy-start.5 = (f32[4]{0:T(128)S(1)}, f32[4]{0:T(128)}, u32[]{:S(2)}) copy-start(f32[4]{0:T(128)} %param.21) | copy-start | bytes 52
  6.5 24.4 %copy-start.3 = (s32[64,4]{0,1:T(4,128)S(1)}, s32[64,4]{0,1:T(4,128)}, u32[]{:S(2)}) copy-start(s32[64,4]{0,1:T(4,128)} %param.25) | copy-start | bytes 3076
  6.5 37.4 %all-to-all-start = ((bf16[64,8,128]{2,1,0:T(8,128)(2,1)}), bf16[64,8,128]{2,1,0:T(8,128)(2,1)S(1)}, u32[]{:S(2)}, u32[]{:S(2)}) async-start(bf16[64,8,128]{2,1,0:T(8,128)(2,1)} %bitcast.65), calls=%async_computation | async-start | bytes 262144 | tf_op jit(solution)/shard_map/all_to_all | solution.py:87
  25.4 103.4 %all-reduce.3.cloned.1.call-start = ((), (), s32[]{:S(2)}) async-start(), calls=%async_computation.3 | async-start | bytes 1507328 | tf_op jit(solution)/shard_map/psum | solution.py:109
  46.0 1.1 copy-start.2
  48.4 0.9 copy-start.1
  49.3 377.6 %all-gather.4.cloned.1.call-start = ((), (), s32[]{:S(2)}) async-start(), calls=%async_computation.4 | async-start | bytes 13271040 | tf_op jit(solution)/shard_map/all_gather | solution.py:137
  195.5 316.9 %all-gather.6.cloned.1.call-start = ((), (), s32[]{:S(2)}) async-start(), calls=%async_computation.5 | async-start | bytes 2119680 | tf_op jit(solution)/shard_map/all_gather | solution.py:149
  443.8 7.9 %copy-start.6 = (bf16[1,2880,180]{1,2,0:T(8,128)(2,1)S(1)}, bf16[1,2880,180]{1,2,0:T(8,128)(2,1)}, u32[]{:S(2)}) copy-start(bf16[1,2880,180]{1,2,0:T(8,128)(2,1)} %param.28) | copy-start | bytes 3110404
  519.6 60.9 %all-to-all-start.2 = ((bf16[64,10,360]{2,1,0:T(8,128)(2,1)}), bf16[64,10,360]{2,1,0:T(8,128)(2,1)S(1)}, u32[]{:S(2)}, u32[]{:S(2)}) async-start(bf16[64,10,360]{2,1,0:T(8,128)(2,1)} %reshape.387), calls=%async_computation.2 | async-start | bytes 1572864 | tf_op jit(solution)/shard_map/all_to_all | solution.py:154
  535.8 2.5 copy-start.4
Sparse Core Ops, SparseCore 0:
  49.4 79.3 all-reduce.2
  195.7 231.1 all-gather.3
  457.0 55.4 all-gather.5
where the time goes:
time: 592 us; the launch traced here: 591 us
  waiting for transfers between devices  419 us (71%)
  blocking collectives  59.9 us (10%)
  local copies, waits for them, and re-layouts  45.1 us (8%)
  starting transfers between devices  35.2 us (6%)
  between operations  14.2 us (2%)
  matrix products  8.63 us (1%)
  other arithmetic  8.61 us (1%)
    all_gather x1, waiting for transfers between devices, on_device(): lax.all_gather(lax.all_to_all(outgoing, 'group', split_axis=0, concat_axi...  231 us
    psum x1, waiting for transfers between devices, on_device(): hidden_state = lax.psum(partial_sum, 'tp')  78.5 us
    all_to_all x1, blocking collectives, on_device(): lax.all_to_all(outgoing, 'group', split_axis=0, concat_axis=0, tiled=True)  59.9 us
    all_gather x1, waiting for transfers between devices, on_device(): joined = lax.all_gather(active, 'tp', axis=1, tiled=True)  55.6 us
    all_to_all x1, waiting for transfers between devices, on_device(): lax.all_to_all(returned, 'group', split_axis=0, concat_axis=0, tiled=True)  42 us
    all_to_all x1, starting transfers between devices, on_device(): lax.all_to_all(remote_pool.reshape(groups, -1, lane_count), 'group', spli...  18.9 us
    all_gather x1, local copies, waits for them, and re-layouts, on_device(): lax.all_gather(lax.all_to_all(outgoing, 'group', split_axis=0, concat_axi...  17 us
    all_to_all x1, starting transfers between devices, on_device(): lax.all_to_all(returned, 'group', split_axis=0, concat_axis=0, tiled=True)  16 us
  transfers between devices with their start and end apart: 5, of which 5 were waited for; matrix products, arithmetic and copies ran while one was open for 2% of the time, Pallas kernels for 0%

commit v1 on v0

--- a/solution.py
+++ b/solution.py
@@ -146,7 +146,9 @@
     gate_val = both[:, :hidden_part]
     up_val = both[:, hidden_part:]
     active = (gate_val * jax.nn.sigmoid(ALPHA * gate_val) * (up_val + 1.0)).astype(jnp.bfloat16)
-    joined = lax.all_gather(active, "tp", axis=1, tiled=True)
+    joined = jnp.concatenate(
+        lax.all_to_all(jnp.stack([active for _ in range(lax.axis_size("tp"))]), "tp", 0, 0), 1
+    )
     result = jnp.dot(joined, expert_down[0], preferred_element_type=jnp.float32).astype(
         jnp.bfloat16
     )

time: 592 us -> 562 us (0.949)
  the two profiles are of different devices: /device:TPU:2 before, /device:TPU:16 now
where the time goes in v1:
time: 562 us; the launch traced here: 561 us
  waiting for transfers between devices  362 us (64%)
  blocking collectives  89.7 us (16%)
  local copies, waits for them, and re-layouts  43.8 us (8%)
  starting transfers between devices  34.5 us (6%)
  between operations  14.5 us (3%)
  matrix products  8.4 us (1%)
  other arithmetic  7.92 us (1%)
    all_gather x1, waiting for transfers between devices, on_device(): lax.all_gather(lax.all_to_all(outgoing, 'group', split_axis=0, concat_axi...  229 us
    psum x1, waiting for transfers between devices, on_device(): hidden_state = lax.psum(partial_sum, 'tp')  81.7 us
    all_to_all x1, blocking collectives, on_device(): lax.all_to_all(outgoing, 'group', split_axis=0, concat_axis=0, tiled=True)  60.3 us
    all_to_all x1, waiting for transfers between devices, on_device(): lax.all_to_all(returned, 'group', split_axis=0, concat_axis=0, tiled=True)  42 us
    all_to_all x1, blocking collectives, on_device(): lax.all_to_all(jnp.stack([active for _ in range(lax.axis_size('tp'))]), '...  29.3 us
    all_to_all x1, starting transfers between devices, on_device(): lax.all_to_all(remote_pool.reshape(groups, -1, lane_count), 'group', spli...  18.7 us
    all_gather x1, local copies, waits for them, and re-layouts, on_device(): lax.all_gather(lax.all_to_all(outgoing, 'group', split_axis=0, concat_axi...  17 us
    all_to_all x1, starting transfers between devices, on_device(): lax.all_to_all(returned, 'group', split_axis=0, concat_axis=0, tiled=True)  15.7 us
  transfers between devices with their start and end apart: 4, of which 4 were waited for; matrix products, arithmetic and copies ran while one was open for 2% of the time, Pallas kernels for 0%

profile of v1, /device:TPU:16, one launch (start us, length us, event | category | flops | bytes accessed | tf_op | source)
XLA Modules:
  0.0 561.2 jit_solution(2948831054669259254)
XLA Ops:
  6.5 18.7 %all-to-all-start = ((bf16[64,8,128]{2,1,0:T(8,128)(2,1)}), bf16[64,8,128]{2,1,0:T(8,128)(2,1)S(1)}, u32[]{:S(2)}, u32[]{:S(2)}) async-start(bf16[64,8,128]{2,1,0:T(8,128)(2,1)} %bitcast.65), calls=%async_computation | async-start | bytes 262144 | tf_op jit(solution)/shard_map/all_to_all | solution.py:87
  26.0 0.9 reshape.400
  26.9 0.8 copy.148
  27.8 0.9 copy.145
  28.8 0.7 add_bitcast_fusion
  31.1 0.8 dynamic_slice.11
  32.3 9.6 %all-to-all-done = bf16[64,8,128]{2,1,0:T(8,128)(2,1)S(1)} async-done(((bf16[64,8,128]{2,1,0:T(8,128)(2,1)}), bf16[64,8,128]{2,1,0:T(8,128)(2,1)S(1)}, u32[]{:S(2)}, u32[]{:S(2)}) %all-to-all-start) | async-done | bytes 131104 | tf_op jit(solution)/shard_map/all_to_all | solution.py:87
  42.1 0.7 slice_maximum_fusion
  43.1 0.4 fusion.39
  44.5 0.6 fusion.40
  45.2 0.9 dynamic_update_slice.3
  46.1 0.9 copy-done.1
  47.2 0.4 select_reduce_fusion
  48.0 81.7 %all-reduce.3.cloned.1.call-done = f32[64,2880]{1,0:T(8,128)} async-done(((f32[64,2880]{1,0:T(8,128)}), f32[64,2880]{1,0:T(8,128)}) %all-reduce.3.cloned.1.call-update) | async-done | bytes 737296 | tf_op jit(solution)/shard_map/psum | solution.py:109
  129.7 1.3 multiply_reduce_fusion
  131.0 1.0 multiply_convert_fusion
  132.0 2.0 gather_fusion
  134.5 60.3 %all_to_all.20 = bf16[64,10,360]{2,1,0:T(8,128)(2,1)S(1)} all-to-all(bf16[64,10,360]{2,1,0:T(8,128)(2,1)S(1)} %bitcast.58), channel_id=1, replica_groups=mesh['group'=64,'tp'=8] {'group'}, dimensions={0} | all-to-all | bytes 921600 | tf_op jit(solution)/shard_map/all_to_all | solution.py:138
  194.8 2.0 copy.166
  196.8 229.1 %all-gather.2.cloned.1.call-done = bf16[64,10,2880]{0,1,2:T(8,128)(2,1)} async-done(((bf16[64,10,360]{0,1,2:T(8,128)(2,1)}), bf16[64,10,2880]{0,1,2:T(8,128)(2,1)}) %all-gather.2.cloned.1.call-update) | async-done | bytes 3686416 | tf_op jit(solution)/shard_map/all_gather | solution.py:137
  425.9 17.0 %copy.167 = bf16[64,10,2880]{2,1,0:T(8,128)(2,1)} copy(bf16[64,10,2880]{0,1,2:T(8,128)(2,1)} %all-gather.2.cloned.1.call-done) | data formatting | bytes 7372800 | tf_op jit(solution)/shard_map/all_gather | solution.py:137
  442.9 7.9 %reshape.394 = bf16[640,2880]{1,0:T(8,128)(2,1)} reshape(bf16[64,10,2880]{2,1,0:T(8,128)(2,1)} %copy.167) | data formatting | bytes 7372800 | tf_op jit(solution)/shard_map/reshape | solution.py:144
  450.7 4.3 fusion
  455.4 29.3 %all_to_all.21 = bf16[8,640,180]{1,2,0:T(8,128)(2,1)S(1)} all-to-all(bf16[8,640,180]{1,2,0:T(8,128)(2,1)S(1)} %stack.2), channel_id=1, replica_groups=mesh['group'=64,'tp'=8] {'tp'}, dimensions={0} | all-to-all | bytes 3686400 | tf_op jit(solution)/shard_map/all_to_all | solution.py:150
  484.7 1.4 reshape.396
  486.1 2.9 convolution_convert_fusion
  489.3 1.1 reshape.397
  490.4 15.7 %all-to-all-start.3 = ((bf16[64,10,360]{2,1,0:T(8,128)(2,1)}), bf16[64,10,360]{2,1,0:T(8,128)(2,1)S(1)}, u32[]{:S(2)}, u32[]{:S(2)}) async-start(bf16[64,10,360]{2,1,0:T(8,128)(2,1)} %reshape.397), calls=%async_computation.3 | async-start | bytes 1572864 | tf_op jit(solution)/shard_map/all_to_all | solution.py:156
  506.3 1.9 gather_fusion.2
  509.0 42.0 %all-to-all-done.3 = bf16[64,10,360]{2,1,0:T(8,128)(2,1)S(1)} async-done(((bf16[64,10,360]{2,1,0:T(8,128)(2,1)}), bf16[64,10,360]{2,1,0:T(8,128)(2,1)S(1)}, u32[]{:S(2)}, u32[]{:S(2)}) %all-to-all-start.3) | async-done | bytes 460832 | tf_op jit(solution)/shard_map/all_to_all | solution.py:156
  551.3 1.0 gather_fusion.1
  552.8 1.6 add_convert_fusion.1
  (85 shorter events, 6.9 us)
Async XLA Ops:
  6.5 38.0 %copy-start = (bf16[256,2880]{0,1:T(8,128)(2,1)S(1)}, bf16[256,2880]{0,1:T(8,128)(2,1)}, u32[]{:S(2)}) copy-start(bf16[256,2880]{0,1:T(8,128)(2,1)} %param.22) | copy-start | bytes 4423684
  6.5 24.0 %copy-start.5 = (f32[4]{0:T(128)S(1)}, f32[4]{0:T(128)}, u32[]{:S(2)}) copy-start(f32[4]{0:T(128)} %param.21) | copy-start | bytes 52
  6.5 24.3 %copy-start.3 = (s32[64,4]{0,1:T(4,128)S(1)}, s32[64,4]{0,1:T(4,128)}, u32[]{:S(2)}) copy-start(s32[64,4]{0,1:T(4,128)} %param.25) | copy-start | bytes 3076
  6.5 35.4 %all-to-all-start = ((bf16[64,8,128]{2,1,0:T(8,128)(2,1)}), bf16[64,8,128]{2,1,0:T(8,128)(2,1)S(1)}, u32[]{:S(2)}, u32[]{:S(2)}) async-start(bf16[64,8,128]{2,1,0:T(8,128)(2,1)} %bitcast.65), calls=%async_computation | async-start | bytes 262144 | tf_op jit(solution)/shard_map/all_to_all | solution.py:87
  25.3 104.4 %all-reduce.3.cloned.1.call-start = ((), (), s32[]{:S(2)}) async-start(), calls=%async_computation.4 | async-start | bytes 1507328 | tf_op jit(solution)/shard_map/psum | solution.py:109
  44.0 1.1 copy-start.2
  46.1 0.9 copy-start.1
  47.0 378.9 %all-gather.2.cloned.1.call-start = ((), (), s32[]{:S(2)}) async-start(), calls=%async_computation.5 | async-start | bytes 13271040 | tf_op jit(solution)/shard_map/all_gather | solution.py:137
  442.9 7.9 %copy-start.6 = (bf16[1,2880,180]{1,2,0:T(8,128)(2,1)S(1)}, bf16[1,2880,180]{1,2,0:T(8,128)(2,1)}, u32[]{:S(2)}) copy-start(bf16[1,2880,180]{1,2,0:T(8,128)(2,1)} %param.28) | copy-start | bytes 3110404
  490.4 60.5 %all-to-all-start.3 = ((bf16[64,10,360]{2,1,0:T(8,128)(2,1)}), bf16[64,10,360]{2,1,0:T(8,128)(2,1)S(1)}, u32[]{:S(2)}, u32[]{:S(2)}) async-start(bf16[64,10,360]{2,1,0:T(8,128)(2,1)} %reshape.397), calls=%async_computation.3 | async-start | bytes 1572864 | tf_op jit(solution)/shard_map/all_to_all | solution.py:156
  506.3 2.5 copy-start.4
Sparse Core Ops, SparseCore 0:
  47.1 82.5 all-reduce.2
  196.9 228.9 all-gather.1
